TPU v7x, 32 devices: a whole 2x2x4 slice. The times are simulated.
32 devices in a mesh: fsdp: 4 (over y, x), ctx: 8 (over z, core).
Axes of the slice: x: 2, y: 2, z: 4, core: 2. Of those that a mesh axis runs over, the one named last changes fastest.
Arguments:
- tokens: bfloat16 [4096, 2048], P(('fsdp', 'ctx')), may hold values from -6 to 6
- w_qkv: bfloat16 [2048, 6144], P(('fsdp', 'ctx')), may hold values from -0.125 to 0.125
- w_out: bfloat16 [2048, 2048], P(('fsdp', 'ctx')), may hold values from -1 to 1
- w_gate_up: bfloat16 [2048, 16384], P(('fsdp', 'ctx')), may hold values from -0.125 to 0.125
- w_down: bfloat16 [8192, 2048], P(('fsdp', 'ctx')), may hold values from -0.0625 to 0.0625
- seq_lengths: int32 [4, 2], P('fsdp'), may hold values from 1 to 768, 1024 in all within a row
- block_order: int32 [4, 8], P('fsdp'), may hold values from 0 to 7, as said below
- cotangent: bfloat16 [4096, 2048], P(('fsdp', 'ctx')), may hold values from -6 to 6
Outputs:
- layer_out: bfloat16 [4096, 2048], P(('fsdp', 'ctx'))
- tokens_grad: float32 [4096, 2048], P(('fsdp', 'ctx'))
- qkv_grad: float32 [2048, 6144], P(('fsdp', 'ctx'))
- out_grad: float32 [2048, 2048], P(('fsdp', 'ctx'))
- gate_up_grad: float32 [2048, 16384], P(('fsdp', 'ctx'))
- down_grad: float32 [8192, 2048], P(('fsdp', 'ctx'))
Inputs may be any that keep to these rules, and one draw needn't show every extreme that they name: `seq_lengths`: the lengths of each group sum to 1024, and none is longer than 768. `block_order`: each row names every block of its group exactly once.
All inputs are finite; a program needn't handle non-finite values.
Results may differ from a plain program's by a relative error of at most 0.018.
Values may be sent and summed in bfloat16 or wider, within the bound.
A program may use at most 704 MiB of HBM per device.

v0:
```python
import jax
import jax.numpy as jnp
from jax import lax
from jax.sharding import PartitionSpec as P

HEADS = 16
HEAD_DIM = 128
BLOCK = 128


def normalize(values):
    average = jnp.mean(values, axis=-1, keepdims=True)
    centered = values - average
    variance = jnp.mean(centered * centered, axis=-1, keepdims=True)
    inv_root = lax.rsqrt(variance + 1e-05)
    return (centered * inv_root, inv_root)


def norm_back(upstream, normed, inv_root):
    first_mean = jnp.mean(upstream, axis=-1, keepdims=True)
    second_mean = jnp.mean(upstream * normed, axis=-1, keepdims=True)
    return inv_root * (upstream - first_mean - normed * second_mean)


def places(token_index, lengths):
    seq_ends = jnp.cumsum(lengths)
    sequence = jnp.sum((token_index[:, None] >= seq_ends[None, :]).astype(jnp.int32), axis=1)
    before = jnp.arange(lengths.shape[0], dtype=jnp.int32)
    seq_start = jnp.sum(jnp.where(before[None, :] < sequence[:, None], lengths[None, :], 0), axis=1)
    return (sequence, token_index - seq_start)


def initial_index(row_index, order_row):
    slot_index = row_index // BLOCK
    slot_table = jnp.arange(order_row.shape[0], dtype=jnp.int32)
    picked = jnp.sum(
        jnp.where(slot_table[None, :] == slot_index[:, None], order_row[None, :], 0), axis=1
    )
    return picked * BLOCK + row_index % BLOCK


def angle_tables(position):
    half_dim = HEAD_DIM // 2
    frequency = 10000.0 ** (-jnp.arange(half_dim, dtype=jnp.float32) * 2.0 / HEAD_DIM)
    angle_table = position.astype(jnp.float32)[:, None] * frequency[None, :]
    angle_table = jnp.concatenate([angle_table, angle_table], axis=-1)
    return (jnp.cos(angle_table)[:, None, :], jnp.sin(angle_table)[:, None, :])


def rotate(values, cosine_table, sine_table):
    half_dim = values.shape[-1] // 2
    turned = jnp.concatenate([-values[..., half_dim:], values[..., :half_dim]], axis=-1)
    return values * cosine_table + turned * sine_table


def unrotate(values, cosine_table, sine_table):
    half_dim = values.shape[-1] // 2
    scaled = values * sine_table
    turned = jnp.concatenate([scaled[..., half_dim:], -scaled[..., :half_dim]], axis=-1)
    return values * cosine_table + turned


def dot(left, right):
    return jnp.dot(left, right, preferred_element_type=jnp.float32)


def times_transposed(left, right):
    return lax.dot_general(
        left, right, (((1,), (1,)), ((), ())), preferred_element_type=jnp.float32
    )


def column_product(left, right):
    return lax.dot_general(
        left, right, (((0,), (0,)), ((), ())), preferred_element_type=jnp.float32
    )


def gather(values, axes):
    return lax.all_gather(values, axes, axis=0, tiled=True)


def scatter(values, axes):
    return lax.psum_scatter(values, axes, scatter_dimension=0, tiled=True)


def spread_columns(weight, outer, parts):
    rows, columns = weight.shape
    inner = columns // (outer * parts)
    pieces = weight.reshape(rows, outer, parts, inner).transpose(2, 0, 1, 3)
    pieces = lax.all_to_all(pieces, "ctx", split_axis=0, concat_axis=0, tiled=True)
    return pieces.reshape(parts * rows, outer * inner)


def collect_rows(grad, outer, parts):
    rows, columns = grad.shape
    inner = columns // outer
    pieces = grad.reshape(parts, rows // parts, columns)
    pieces = lax.all_to_all(pieces, "ctx", split_axis=0, concat_axis=0, tiled=True)
    pieces = pieces.reshape(parts, rows // parts, outer, inner).transpose(1, 2, 0, 3)
    return pieces.reshape(rows // parts, outer * parts * inner).astype(jnp.float32)


def per_device(tokens, w_qkv, w_out, w_gate_up, w_down, seq_lengths, block_order, cotangent):
    lengths = seq_lengths[0]
    order_row = block_order[0]
    parts = lax.axis_size("ctx")
    groups = lax.axis_size("fsdp")
    rows, width = tokens.shape
    length = rows * parts
    heads = HEADS // parts
    head_width = heads * HEAD_DIM
    low = jnp.bfloat16
    score_scale = HEAD_DIM ** (-0.5)
    qkv_cols = gather(spread_columns(w_qkv, 3, parts), "fsdp")
    out_full = gather(w_out, ("fsdp", "ctx"))
    gate_up_cols = gather(spread_columns(w_gate_up, 2 * groups, parts), "fsdp")
    down_rows = gather(w_down, "fsdp")
    cot_full = gather(cotangent, "ctx")
    inputs = tokens.astype(jnp.float32)
    normed_in, root_in = normalize(inputs)
    normed_in_full = gather(normed_in.astype(low), "ctx")
    row_index = jnp.arange(length, dtype=jnp.int32)
    seq, pos = places(initial_index(row_index, order_row), lengths)
    cosine_table, sine_table = angle_tables(pos)
    allowed = ((seq[:, None] == seq[None, :]) & (pos[None, :] <= pos[:, None]))[None]
    qkv = dot(normed_in_full, qkv_cols)
    head_shape = (length, heads, HEAD_DIM)
    queries = rotate(qkv[:, :head_width].reshape(head_shape), cosine_table, sine_table).astype(low)
    keys = rotate(
        qkv[:, head_width : 2 * head_width].reshape(head_shape), cosine_table, sine_table
    ).astype(low)
    values = qkv[:, 2 * head_width :].astype(low).reshape(head_shape)
    scores = jnp.einsum("qhd,khd->hqk", queries, keys, preferred_element_type=jnp.float32)
    scores = jnp.where(allowed, scores * score_scale, -1e30)
    row_max = jnp.max(scores, axis=-1)
    weights = jnp.where(allowed, jnp.exp(scores - row_max[..., None]), 0.0)
    row_total = jnp.sum(weights, axis=-1)
    mixed = jnp.einsum(
        "hqk,khd->qhd", weights.astype(low), values, preferred_element_type=jnp.float32
    )
    log_total = row_max + jnp.log(row_total)
    attn_heads = mixed / jnp.transpose(row_total)[..., None]
    mix_pieces = attn_heads.astype(low).reshape(parts, rows, head_width)
    mix_pieces = lax.all_to_all(mix_pieces, "ctx", split_axis=0, concat_axis=0, tiled=True)
    mix_low = mix_pieces.transpose(1, 0, 2).reshape(rows, width)
    residual = inputs + dot(mix_low, out_full)
    normed_mid, root_mid = normalize(residual)
    normed_mid_full = gather(normed_mid.astype(low), "ctx")
    gate_up = dot(normed_mid_full, gate_up_cols)
    units = gate_up.shape[1] // 2
    gate_part = gate_up[:, :units]
    up_part = gate_up[:, units:]
    sigmoid_gate = jax.nn.sigmoid(gate_part)
    silu_gate = gate_part * sigmoid_gate
    activated = (silu_gate * up_part).astype(low)
    down_out = scatter(dot(activated, down_rows).astype(low), "ctx")
    layer_out = (residual + down_out.astype(jnp.float32)).astype(low)
    down_grad = scatter(column_product(activated, cot_full).astype(low), "fsdp").astype(jnp.float32)
    act_grad = times_transposed(cot_full, down_rows)
    gate_grad = act_grad * up_part * sigmoid_gate * (1.0 + gate_part * (1.0 - sigmoid_gate))
    up_grad = act_grad * silu_gate
    gate_up_back = jnp.concatenate([gate_grad, up_grad], axis=1).astype(low)
    mid_back = scatter(times_transposed(gate_up_back, gate_up_cols).astype(low), "ctx")
    gate_up_grad = scatter(column_product(normed_mid_full, gate_up_back).astype(low), "fsdp")
    residual_back = cotangent.astype(jnp.float32) + norm_back(
        mid_back.astype(jnp.float32), normed_mid, root_mid
    )
    proj_back = residual_back.astype(low)
    mix_back = times_transposed(proj_back, out_full).astype(low)
    out_grad = scatter(column_product(mix_low, proj_back).astype(low), ("fsdp", "ctx"))
    back_pieces = mix_back.reshape(rows, parts, head_width).transpose(1, 0, 2)
    back_pieces = lax.all_to_all(back_pieces, "ctx", split_axis=0, concat_axis=0, tiled=True)
    back_heads = back_pieces.reshape(head_shape)
    delta = jnp.einsum("qhd,qhd->hq", back_heads.astype(jnp.float32), attn_heads)
    probs = jnp.where(allowed, jnp.exp(scores - log_total[..., None]), 0.0)
    value_back = jnp.einsum(
        "hqk,qhd->khd", probs.astype(low), back_heads, preferred_element_type=jnp.float32
    )
    prob_back = jnp.einsum("qhd,khd->hqk", back_heads, values, preferred_element_type=jnp.float32)
    score_back = (score_scale * probs * (prob_back - delta[..., None])).astype(low)
    query_back = jnp.einsum("hqk,khd->qhd", score_back, keys, preferred_element_type=jnp.float32)
    key_back = jnp.einsum("hqk,qhd->khd", score_back, queries, preferred_element_type=jnp.float32)
    qkv_back = jnp.concatenate(
        [
            unrotate(query_back, cosine_table, sine_table).reshape(length, head_width),
            unrotate(key_back, cosine_table, sine_table).reshape(length, head_width),
            value_back.reshape(length, head_width),
        ],
        axis=1,
    ).astype(low)
    in_back = scatter(times_transposed(qkv_back, qkv_cols).astype(low), "ctx")
    tokens_grad = residual_back + norm_back(in_back.astype(jnp.float32), normed_in, root_in)
    qkv_grad = scatter(column_product(normed_in_full, qkv_back).astype(low), "fsdp")
    return (
        layer_out,
        tokens_grad,
        collect_rows(qkv_grad, 3, parts),
        out_grad.astype(jnp.float32),
        collect_rows(gate_up_grad, 2 * groups, parts),
        down_grad,
    )


def solution(mesh):
    both = P(("fsdp", "ctx"), None)
    one = P("fsdp", None)
    return jax.shard_map(
        per_device,
        mesh=mesh,
        in_specs=(both, both, both, both, both, one, one, both),
        out_specs=(both,) * 6,
        check_vma=False,
    )
```

profile of v0, /device:TPU:0, one launch (start us, length us, event | category | flops | bytes accessed | tf_op | source)
XLA Modules:
  0.0 1039.7 jit_solution(7652950163884755804)
XLA Ops:
  8.7 27.2 %all_to_all.30 = bf16[8,64,3,256]{3,1,2,0:T(8,128)(2,1)S(1)} all-to-all(bf16[8,64,3,256]{3,1,2,0:T(8,128)(2,1)S(1)} %copy.97), channel_id=1, replica_groups=mesh['fsdp'=4,'ctx'=8] {'ctx'}, dimensions={0} | all-to-all | bytes 1572864 | tf_op jit(solution)/shard_map/all_to_all | solution.py:91
  41.9 51.5 %all_to_all.31 = bf16[8,64,8,256]{3,2,1,0:T(8,128)(2,1)S(1)} all-to-all(bf16[8,64,8,256]{3,2,1,0:T(8,128)(2,1)S(1)} %bitcast.108), channel_id=1, replica_groups=mesh['fsdp'=4,'ctx'=8] {'ctx'}, dimensions={0} | all-to-all | bytes 4194304 | tf_op jit(solution)/shard_map/all_to_all | solution.py:91
  99.5 30.2 %all-gather.8.cloned.1.call-done = bf16[1024,2048]{1,0:T(8,128)(2,1)} async-done(((bf16[128,2048]{1,0:T(8,128)(2,1)}), bf16[1024,2048]{1,0:T(8,128)(2,1)}) %all-gather.8.cloned.1.call-update) | async-done | bytes 4194320 | tf_op jit(solution)/shard_map/all_gather | solution.py:80
  146.3 23.3 %all_to_all.32 = bf16[8,128,256]{1,2,0:T(8,128)(2,1)S(1)} all-to-all(bf16[8,128,256]{1,2,0:T(8,128)(2,1)S(1)} %copy.102), channel_id=1, replica_groups=mesh['fsdp'=4,'ctx'=8] {'ctx'}, dimensions={0} | all-to-all | bytes 1048576 | tf_op jit(solution)/shard_map/all_to_all | solution.py:145
  169.6 40.8 %all-gather.12.cloned.1.call-done = bf16[2048,2048]{1,0:T(8,128)(2,1)} async-done(((bf16[64,2048]{1,0:T(8,128)(2,1)}), bf16[2048,2048]{1,0:T(8,128)(2,1)}) %all-gather.12.cloned.1.call-update) | async-done | bytes 8388624 | tf_op jit(solution)/shard_map/all_gather | solution.py:80
  218.4 80.4 %all-gather.16.cloned.1.call-done = bf16[2048,2048]{1,0:T(8,128)(2,1)} async-done(((bf16[512,2048]{1,0:T(8,128)(2,1)}), bf16[2048,2048]{1,0:T(8,128)(2,1)}) %all-gather.16.cloned.1.call-update) | async-done | bytes 8388624 | tf_op jit(solution)/shard_map/all_gather | solution.py:80
  298.8 48.9 %all-gather.14.cloned.1.call-done = bf16[1024,2048]{1,0:T(8,128)(2,1)} async-done(((bf16[128,2048]{1,0:T(8,128)(2,1)}), bf16[1024,2048]{1,0:T(8,128)(2,1)}) %all-gather.14.cloned.1.call-update) | async-done | bytes 4194320 | tf_op jit(solution)/shard_map/all_gather | solution.py:80
  347.7 14.5 %fusion.74 = f32[1024,2048]{1,0:T(8,128)} fusion(bf16[1024,2048]{1,0:T(8,128)(2,1)} %all-gather.14.cloned.1.call-done, bf16[2048,2048]{1,0:T(8,128)(2,1)} %all-gather.16.cloned.1.call-done), kind=kOutput, calls=%fused_computation.131 | convolution fusion | flops 8589934592 | bytes 20971520 | tf_op jit(solution)/shard_map/dot_general | solution.py:64
  362.3 38.6 %all-gather.18.cloned.1.call-done = bf16[1024,2048]{1,0:T(8,128)(2,1)} async-done(((bf16[256,2048]{1,0:T(8,128)(2,1)}), bf16[1024,2048]{1,0:T(8,128)(2,1)}) %all-gather.18.cloned.1.call-update) | async-done | bytes 4194320 | tf_op jit(solution)/shard_map/all_gather | solution.py:80
  400.8 48.5 %all-gather.20.cloned.1.call-done = bf16[1024,2048]{1,0:T(8,128)(2,1)} async-done(((bf16[128,2048]{1,0:T(8,128)(2,1)}), bf16[1024,2048]{1,0:T(8,128)(2,1)}) %all-gather.20.cloned.1.call-update) | async-done | bytes 4194320 | tf_op jit(solution)/shard_map/all_gather | solution.py:80
  449.3 13.1 %multiply_convert_fusion.2 = (bf16[1024,1024]{1,0:T(8,128)(2,1)S(1)}, bf16[1024,1024]{1,0:T(8,128)(2,1)S(1)}, bf16[1024,1024]{1,0:T(8,128)(2,1)}) fusion(f32[1024,2048]{1,0:T(8,128)} %fusion.74, bf16[1024,2048]{1,0:T(8,128)(2,1)} %all-gather.20.cloned.1.call-done, bf16[1024,2048]{1,0:T(8,128)(2,1)} %all-gather.18.cloned.1.call-done), kind=kOutput, calls=%fused_computation.12 | convolution fusion | flops 4310695936 | bytes 23068672 | tf_op jit(solution)/shard_map/dot_general | solution.py:68
  464.5 12.6 %convolution_convert_fusion.2 = bf16[1024,2048]{1,0:T(8,128)(2,1)} fusion(bf16[2048,2048]{1,0:T(8,128)(2,1)} %all-gather.16.cloned.1.call-done, bf16[1024,1024]{1,0:T(8,128)(2,1)S(1)} %get-tuple-element.13, bf16[1024,1024]{1,0:T(8,128)(2,1)S(1)} %get-tuple-element.12), kind=kOutput, calls=%fused_computation.21 | convolution fusion | flops 8600420352 | bytes 16777216 | tf_op jit(solution)/shard_map/dot_general | solution.py:68
  477.3 9.3 convolution_convert_fusion.5
  486.6 39.4 %reduce-scatter.10.cloned.1.call-done = bf16[128,2048]{1,0:T(8,128)(2,1)} async-done(((bf16[1024,2048]{1,0:T(8,128)(2,1)}), bf16[128,2048]{1,0:T(8,128)(2,1)}) %reduce-scatter.10.cloned.1.call-update) | async-done | bytes 524304 | tf_op jit(solution)/shard_map/reduce_scatter | solution.py:84
  527.4 49.3 %reduce-scatter.8.cloned.1.call-done = bf16[128,2048]{1,0:T(8,128)(2,1)} async-done(((bf16[1024,2048]{1,0:T(8,128)(2,1)}), bf16[128,2048]{1,0:T(8,128)(2,1)}) %reduce-scatter.8.cloned.1.call-update) | async-done | bytes 524304 | tf_op jit(solution)/shard_map/reduce_scatter | solution.py:84
  579.4 7.1 convolution_convert_fusion.7
  592.8 15.3 %all-to-all-done.3 = bf16[8,128,256]{1,2,0:T(8,128)(2,1)} async-done(((bf16[8,128,256]{1,2,0:T(8,128)(2,1)}), bf16[8,128,256]{1,2,0:T(8,128)(2,1)}, u32[]{:S(2)}, u32[]{:S(2)}) %all-to-all-start.3) | async-done | bytes 524320 | tf_op jit(solution)/shard_map/all_to_all | solution.py:173
  636.7 14.0 %convolution_convert_fusion = bf16[2048,2048]{1,0:T(8,128)(2,1)} fusion(bf16[1024,2048]{1,0:T(8,128)(2,1)} %all-gather.14.cloned.1.call-done, bf16[1024,1024]{1,0:T(8,128)(2,1)} %copy-done.25, bf16[1024,1024]{1,0:T(8,128)(2,1)} %copy-done.24), kind=kOutput, calls=%fused_computation.4 | convolution fusion | flops 8602517504 | bytes 16777216 | tf_op jit(solution)/shard_map/dot_general | solution.py:74
  650.8 9.6 convolution_convert_fusion.4
  660.8 7.6 convolution_convert_fusion.3
  684.0 84.8 %reduce-scatter.18.cloned.1.call-done = bf16[512,2048]{1,0:T(8,128)(2,1)} async-done(((bf16[2048,2048]{1,0:T(8,128)(2,1)}), bf16[512,2048]{1,0:T(8,128)(2,1)}) %reduce-scatter.18.cloned.1.call-update) | async-done | bytes 2097168 | tf_op jit(solution)/shard_map/reduce_scatter | solution.py:84
  773.6 50.6 %reduce-scatter.20.cloned.1.call-done = bf16[256,2048]{1,0:T(8,128)(2,1)} async-done(((bf16[1024,2048]{1,0:T(8,128)(2,1)}), bf16[256,2048]{1,0:T(8,128)(2,1)}) %reduce-scatter.20.cloned.1.call-update) | async-done | bytes 1048592 | tf_op jit(solution)/shard_map/reduce_scatter | solution.py:84
  833.0 44.0 %reduce-scatter.12.cloned.1.call-done = bf16[128,2048]{1,0:T(8,128)(2,1)} async-done(((bf16[1024,2048]{1,0:T(8,128)(2,1)}), bf16[128,2048]{1,0:T(8,128)(2,1)}) %reduce-scatter.12.cloned.1.call-update) | async-done | bytes 524304 | tf_op jit(solution)/shard_map/reduce_scatter | solution.py:84
  889.9 141.4 %reduce-scatter.16.cloned.1.call-done = bf16[64,2048]{1,0:T(8,128)(2,1)} async-done(((bf16[2048,2048]{1,0:T(8,128)(2,1)}), bf16[64,2048]{1,0:T(8,128)(2,1)}) %reduce-scatter.16.cloned.1.call-update) | async-done | bytes 262160 | tf_op jit(solution)/shard_map/reduce_scatter | solution.py:84
  (155 shorter events, 123.1 us)
Async XLA Ops:
  7.2 92.3 %all-gather.10.cloned.1.call-start = ((), (), s32[]{:S(2)}) async-start(), calls=%async_computation.14 | async-start | bytes 3932160 | tf_op jit(solution)/shard_map/all_gather | solution.py:80
  8.5 29.2 %copy-start = (bf16[128,2048]{1,0:T(8,128)(2,1)S(1)}, bf16[128,2048]{1,0:T(8,128)(2,1)}, u32[]{:S(2)}) copy-start(bf16[128,2048]{1,0:T(8,128)(2,1)} %param.8) | copy-start | bytes 1572868
  8.7 32.2 %copy-start.11 = (bf16[64,16384]{1,0:T(8,128)(2,1)S(1)}, bf16[64,16384]{1,0:T(8,128)(2,1)}, u32[]{:S(2)}) copy-start(bf16[64,16384]{1,0:T(8,128)(2,1)} %param.11) | copy-start | bytes 6291460
  37.7 92.0 %all-gather.8.cloned.1.call-start = ((), (), s32[]{:S(2)}) async-start(), calls=%async_computation.13 | async-start | bytes 4718592 | tf_op jit(solution)/shard_map/all_gather | solution.py:80
  40.2 170.3 %all-gather.12.cloned.1.call-start = ((), (), s32[]{:S(2)}) async-start(), calls=%async_computation.15 | async-start | bytes 8650752 | tf_op jit(solution)/shard_map/all_gather | solution.py:80
  40.9 257.9 %all-gather.16.cloned.1.call-start = ((), (), s32[]{:S(2)}) async-start(), calls=%async_computation.17 | async-start | bytes 10485760 | tf_op jit(solution)/shard_map/all_gather | solution.py:80
  95.5 252.3 %all-gather.14.cloned.1.call-start = ((), (), s32[]{:S(2)}) async-start(), calls=%async_computation.16 | async-start | bytes 4718592 | tf_op jit(solution)/shard_map/all_gather | solution.py:80
  98.3 38.2 %copy-start.1 = (f32[1024,128]{0,1:T(8,128)}, f32[1024,128]{0,1:T(8,128)S(1)}, u32[]{:S(2)}) copy-start(f32[1024,128]{0,1:T(8,128)S(1)} %get-tuple-element.34) | copy-start | bytes 1572868
  98.3 38.2 %copy-start.4 = (f32[1024,128]{0,1:T(8,128)}, f32[1024,128]{0,1:T(8,128)S(1)}, u32[]{:S(2)}) copy-start(f32[1024,128]{0,1:T(8,128)S(1)} %get-tuple-element.33) | copy-start | bytes 1572868
  99.5 42.0 %copy-start.6 = (pred[1024,1024]{0,1:T(8,128)(4,1)}, pred[1024,1024]{0,1:T(8,128)(4,1)S(1)}, u32[]{:S(2)}) copy-start(pred[1024,1024]{0,1:T(8,128)(4,1)S(1)} %compare_and_fusion) | copy-start | bytes 3145732
  216.4 184.4 %all-gather.18.cloned.1.call-start = ((), (), s32[]{:S(2)}) async-start(), calls=%async_computation.18 | async-start | bytes 5242880 | tf_op jit(solution)/shard_map/all_gather | solution.py:80
  217.0 232.3 %all-gather.20.cloned.1.call-start = ((), (), s32[]{:S(2)}) async-start(), calls=%async_computation.20 | async-start | bytes 4718592 | tf_op jit(solution)/shard_map/all_gather | solution.py:80
  217.8 308.2 %reduce-scatter.10.cloned.1.call-start = ((), (), s32[]{:S(2)}) async-start(), calls=%async_computation.21 | async-start | bytes 4718592 | tf_op jit(solution)/shard_map/reduce_scatter | solution.py:84
  477.1 99.6 %reduce-scatter.8.cloned.1.call-start = ((), (), s32[]{:S(2)}) async-start(), calls=%async_computation.19 | async-start | bytes 4718592 | tf_op jit(solution)/shard_map/reduce_scatter | solution.py:84
  588.6 19.5 %all-to-all-start.3 = ((bf16[8,128,256]{1,2,0:T(8,128)(2,1)}), bf16[8,128,256]{1,2,0:T(8,128)(2,1)}, u32[]{:S(2)}, u32[]{:S(2)}) async-start(bf16[8,128,256]{1,2,0:T(8,128)(2,1)} %bitcast.118), calls=%async_computation.5 | async-start | bytes 1048576 | tf_op jit(solution)/shard_map/all_to_all | solution.py:173
  592.7 86.6 %reduce-scatter.14.cloned.1.call-start = ((), (), s32[]{:S(2)}) async-start(), calls=%async_computation.23 | async-start | bytes 3932160 | tf_op jit(solution)/shard_map/reduce_scatter | solution.py:84
  636.4 132.4 %reduce-scatter.18.cloned.1.call-start = ((), (), s32[]{:S(2)}) async-start(), calls=%async_computation.25 | async-start | bytes 10485760 | tf_op jit(solution)/shard_map/reduce_scatter | solution.py:84
  650.7 173.5 %reduce-scatter.20.cloned.1.call-start = ((), (), s32[]{:S(2)}) async-start(), calls=%async_computation.26 | async-start | bytes 5242880 | tf_op jit(solution)/shard_map/reduce_scatter | solution.py:84
  660.3 216.7 %reduce-scatter.12.cloned.1.call-start = ((), (), s32[]{:S(2)}) async-start(), calls=%async_computation.22 | async-start | bytes 4718592 | tf_op jit(solution)/shard_map/reduce_scatter | solution.py:84
  668.4 362.8 %reduce-scatter.16.cloned.1.call-start = ((), (), s32[]{:S(2)}) async-start(), calls=%async_computation.24 | async-start | bytes 8650752 | tf_op jit(solution)/shard_map/reduce_scatter | solution.py:84
  679.4 89.4 %all-to-all-start.4 = ((bf16[8,64,768]{2,1,0:T(8,128)(2,1)}), bf16[8,64,768]{2,1,0:T(8,128)(2,1)S(1)}, u32[]{:S(2)}, u32[]{:S(2)}) async-start(bf16[8,64,768]{2,1,0:T(8,128)(2,1)} %bitcast.122), calls=%async_computation.8 | async-start | bytes 1572864 | tf_op jit(solution)/shard_map/all_to_all | solution.py:99
  768.8 112.2 %all-to-all-start.5 = ((bf16[8,64,2048]{2,1,0:T(8,128)(2,1)}), bf16[8,64,2048]{2,1,0:T(8,128)(2,1)}, u32[]{:S(2)}, u32[]{:S(2)}) async-start(bf16[8,64,2048]{2,1,0:T(8,128)(2,1)} %bitcast.117), calls=%async_computation.11 | async-start | bytes 4194304 | tf_op jit(solution)/shard_map/all_to_all | solution.py:99
  827.0 50.0 %copy-start.17 = (f32[128]{0:T(128)S(1)}, f32[128]{0:T(128)}, u32[]{:S(2)}) copy-start(f32[128]{0:T(128)} %copy-done.16) | copy-start | bytes 1540
  827.0 50.0 %copy-start.19 = (f32[128]{0:T(128)S(1)}, f32[128]{0:T(128)}, u32[]{:S(2)}) copy-start(f32[128]{0:T(128)} %copy-done.18) | copy-start | bytes 1540
  (19 other events, 85.7 us)
Sparse Core Ops, SparseCore 0:
  37.8 42.7 all-gather.9
  82.8 46.8 all-gather.7
  132.7 77.6 all-gather.11
  212.7 86.0 all-gather.15
  300.8 46.8 all-gather.13
  349.4 51.3 all-gather.17
  402.4 46.8 all-gather.19
  477.2 48.7 reduce-scatter.9
  528.3 48.3 reduce-scatter.7
  636.5 42.7 reduce-scatter.13
  682.4 86.3 reduce-scatter.17
  771.6 52.5 reduce-scatter.19
  827.1 49.8 reduce-scatter.11
  879.2 151.9 reduce-scatter.15
where the time goes:
time: 1040 us
  waiting for transfers between devices  720 us (69%)
  matrix products  130 us (12%)
  blocking collectives  102 us (10%)
  local copies, waits for them, and re-layouts  33.2 us (3%)
  other arithmetic  24.4 us (2%)
  starting transfers between devices  15.8 us (2%)
  between operations  14.7 us (1%)
    reduce_scatter x7, waiting for transfers between devices, scatter(): return lax.psum_scatter(values, axes, scatter_dimension=0, tiled=True)  415 us
    all_gather x7, waiting for transfers between devices, gather(): return lax.all_gather(values, axes, axis=0, tiled=True)  287 us
    all_to_all x2, blocking collectives, spread_columns(): lax.all_to_all(pieces, 'ctx', split_axis=0, concat_axis=0, tiled=True)  78.7 us
    dot_general x4, matrix products, times_transposed(): lax.dot_general(left, right, (((1,), (1,)), ((), ())), preferred_element_...  40.4 us
    dot_general x4, matrix products, dot(): return jnp.dot(left, right, preferred_element_type=jnp.float32)  34.8 us
    dot_general x4, matrix products, column_product(): lax.dot_general(left, right, (((0,), (0,)), ((), ())), preferred_element_...  34 us
    all_to_all x1, blocking collectives, per_device(): lax.all_to_all(mix_pieces, 'ctx', split_axis=0, concat_axis=0, tiled=True)  23.3 us
  transfers between devices with their start and end apart: 17, of which 14 were waited for; matrix products, arithmetic and copies ran while one was open for 11% of the time, Pallas kernels for 0%

commit v1 on v0

--- a/solution.py
+++ b/solution.py
@@ -6,6 +6,17 @@
 HEADS = 16
 HEAD_DIM = 128
 BLOCK = 128
+
+
+def cut_along(shard, dim, size):
+    before, after = (shard.shape[:dim], shard.shape[dim + 1 :])
+    return jnp.moveaxis(shard.reshape(*before, size, -1, *after), dim, 0)
+
+
+def in_order(blocks, dim):
+    blocks = jnp.moveaxis(blocks, 0, dim)
+    shape = blocks.shape
+    return blocks.reshape(*shape[:dim], shape[dim] * shape[dim + 1], *shape[dim + 2 :])
 
 
 def normalize(values):
@@ -142,7 +153,16 @@
     log_total = row_max + jnp.log(row_total)
     attn_heads = mixed / jnp.transpose(row_total)[..., None]
     mix_pieces = attn_heads.astype(low).reshape(parts, rows, head_width)
-    mix_pieces = lax.all_to_all(mix_pieces, "ctx", split_axis=0, concat_axis=0, tiled=True)
+    length_2, index = (lax.axis_size("ctx"), lax.axis_index("ctx"))
+    blocks = cut_along(mix_pieces, 0, length_2)
+    outs = [blocks[index]]
+    for step in range(1, length_2):
+        sent = blocks[(index + step) % length_2]
+        outs.append(
+            lax.ppermute(sent, "ctx", [(i, (i + step) % length_2) for i in range(length_2)])
+        )
+    blocks = jnp.stack(outs)[(index - jnp.arange(length_2)) % length_2]
+    mix_pieces = in_order(blocks, 0)
     mix_low = mix_pieces.transpose(1, 0, 2).reshape(rows, width)
     residual = inputs + dot(mix_low, out_full)
     normed_mid, root_mid = normalize(residual)

time: 1040 us -> 1040 us (level)
  blocking collectives: 102 us -> 78.7 us
  starting transfers between devices: 15.8 us -> 32.3 us
    all_to_all x1 -> x0, blocking collectives: 23.3 us -> none  [per_device(): lax.all_to_all(mix_pieces, 'ctx', split_axis=0, concat_axis=0, tiled=True)]
    ppermute x0 -> x7, starting transfers between devices: none -> 16.9 us  [per_device(): lax.ppermute(sent, 'ctx', [(i, (i + step) % length_2) for i in range(leng...]
  transfers between devices with their start and end apart: 17 -> 24, of which waited for: 14 -> 17; matrix products, arithmetic and copies ran while one was open for 11% -> 11% of each run, Pallas kernels for 0% -> 0%
where the time goes in v1:
time: 1040 us
  waiting for transfers between devices  723 us (70%)
  matrix products  130 us (12%)
  blocking collectives  78.7 us (8%)
  local copies, waits for them, and re-layouts  36 us (3%)
  starting transfers between devices  32.3 us (3%)
  other arithmetic  24.4 us (2%)
  between operations  15 us (1%)
    reduce_scatter x7, waiting for transfers between devices, scatter(): return lax.psum_scatter(values, axes, scatter_dimension=0, tiled=True)  414 us
    all_gather x7, waiting for transfers between devices, gather(): return lax.all_gather(values, axes, axis=0, tiled=True)  286 us
    all_to_all x2, blocking collectives, spread_columns(): lax.all_to_all(pieces, 'ctx', split_axis=0, concat_axis=0, tiled=True)  78.7 us
    dot_general x4, matrix products, times_transposed(): lax.dot_general(left, right, (((1,), (1,)), ((), ())), preferred_element_...  40.4 us
    dot_general x4, matrix products, dot(): return jnp.dot(left, right, preferred_element_type=jnp.float32)  34.8 us
    dot_general x4, matrix products, column_product(): lax.dot_general(left, right, (((0,), (0,)), ((), ())), preferred_element_...  34 us
  transfers between devices with their start and end apart: 24, of which 17 were waited for; matrix products, arithmetic and copies ran while one was open for 11% of the time, Pallas kernels for 0%

profile of v1, /device:TPU:0, one launch (start us, length us, event | category | flops | bytes accessed | tf_op | source)
XLA Modules:
  0.0 1039.5 jit_solution(6426174295951111515)
XLA Ops:
  8.7 27.2 %all_to_all.25 = bf16[8,64,3,256]{3,1,2,0:T(8,128)(2,1)S(1)} all-to-all(bf16[8,64,3,256]{3,1,2,0:T(8,128)(2,1)S(1)} %copy.157), channel_id=1, replica_groups=mesh['fsdp'=4,'ctx'=8] {'ctx'}, dimensions={0} | all-to-all | bytes 1572864 | tf_op jit(solution)/shard_map/all_to_all | solution.py:102
  41.8 51.5 %all_to_all.26 = bf16[8,64,8,256]{3,2,1,0:T(8,128)(2,1)S(1)} all-to-all(bf16[8,64,8,256]{3,2,1,0:T(8,128)(2,1)S(1)} %bitcast.146), channel_id=1, replica_groups=mesh['fsdp'=4,'ctx'=8] {'ctx'}, dimensions={0} | all-to-all | bytes 4194304 | tf_op jit(solution)/shard_map/all_to_all | solution.py:102
  99.6 30.1 %all-gather.8.cloned.1.call-done = bf16[1024,2048]{1,0:T(8,128)(2,1)} async-done(((bf16[128,2048]{1,0:T(8,128)(2,1)}), bf16[1024,2048]{1,0:T(8,128)(2,1)}) %all-gather.8.cloned.1.call-update) | async-done | bytes 4194320 | tf_op jit(solution)/shard_map/all_gather | solution.py:91
  156.7 11.0 %collective-permute-start.6 = (bf16[1,128,256]{2,1,0:T(8,128)(2,1)S(1)}, bf16[1,128,256]{2,1,0:T(8,128)(2,1)S(1)}, u32[]{:S(2)}, u32[]{:S(2)}) collective-permute-start(bf16[1,128,256]{2,1,0:T(8,128)(2,1)S(1)} %bitcast.170), channel_id=1, source_target_pairs={{0,7},{1,0},{2,1},{3,2},{4,3},{5,4},{6,5},{7,6},{8,15},{9,8},{10,9... | collective-permute-start | bytes 196616 | tf_op jit(solution)/shard_map/ppermute | solution.py:162
  171.4 38.9 %all-gather.12.cloned.1.call-done = bf16[2048,2048]{1,0:T(8,128)(2,1)} async-done(((bf16[64,2048]{1,0:T(8,128)(2,1)}), bf16[2048,2048]{1,0:T(8,128)(2,1)}) %all-gather.12.cloned.1.call-update) | async-done | bytes 8388624 | tf_op jit(solution)/shard_map/all_gather | solution.py:91
  217.6 81.0 %all-gather.16.cloned.1.call-done = bf16[2048,2048]{1,0:T(8,128)(2,1)} async-done(((bf16[512,2048]{1,0:T(8,128)(2,1)}), bf16[2048,2048]{1,0:T(8,128)(2,1)}) %all-gather.16.cloned.1.call-update) | async-done | bytes 8388624 | tf_op jit(solution)/shard_map/all_gather | solution.py:91
  298.6 48.9 %all-gather.14.cloned.1.call-done = bf16[1024,2048]{1,0:T(8,128)(2,1)} async-done(((bf16[128,2048]{1,0:T(8,128)(2,1)}), bf16[1024,2048]{1,0:T(8,128)(2,1)}) %all-gather.14.cloned.1.call-update) | async-done | bytes 4194320 | tf_op jit(solution)/shard_map/all_gather | solution.py:91
  347.6 14.5 %fusion.76 = f32[1024,2048]{1,0:T(8,128)} fusion(bf16[1024,2048]{1,0:T(8,128)(2,1)} %all-gather.14.cloned.1.call-done, bf16[2048,2048]{1,0:T(8,128)(2,1)} %all-gather.16.cloned.1.call-done), kind=kOutput, calls=%fused_computation.155 | convolution fusion | flops 8589934592 | bytes 20971520 | tf_op jit(solution)/shard_map/dot_general | solution.py:75
  362.1 38.6 %all-gather.18.cloned.1.call-done = bf16[1024,2048]{1,0:T(8,128)(2,1)} async-done(((bf16[256,2048]{1,0:T(8,128)(2,1)}), bf16[1024,2048]{1,0:T(8,128)(2,1)}) %all-gather.18.cloned.1.call-update) | async-done | bytes 4194320 | tf_op jit(solution)/shard_map/all_gather | solution.py:91
  400.7 48.5 %all-gather.20.cloned.1.call-done = bf16[1024,2048]{1,0:T(8,128)(2,1)} async-done(((bf16[128,2048]{1,0:T(8,128)(2,1)}), bf16[1024,2048]{1,0:T(8,128)(2,1)}) %all-gather.20.cloned.1.call-update) | async-done | bytes 4194320 | tf_op jit(solution)/shard_map/all_gather | solution.py:91
  449.2 13.1 %multiply_convert_fusion.2 = (bf16[1024,1024]{1,0:T(8,128)(2,1)S(1)}, bf16[1024,1024]{1,0:T(8,128)(2,1)S(1)}, bf16[1024,1024]{1,0:T(8,128)(2,1)}) fusion(f32[1024,2048]{1,0:T(8,128)} %fusion.76, bf16[1024,2048]{1,0:T(8,128)(2,1)} %all-gather.20.cloned.1.call-done, bf16[1024,2048]{1,0:T(8,128)(2,1)} %all-gather.18.cloned.1.call-done), kind=kOutput, calls=%fused_computation.13 | convolution fusion | flops 4310695936 | bytes 23068672 | tf_op jit(solution)/shard_map/dot_general | solution.py:79
  464.3 12.6 %convolution_convert_fusion.2 = bf16[1024,2048]{1,0:T(8,128)(2,1)} fusion(bf16[2048,2048]{1,0:T(8,128)(2,1)} %all-gather.16.cloned.1.call-done, bf16[1024,1024]{1,0:T(8,128)(2,1)S(1)} %get-tuple-element.13, bf16[1024,1024]{1,0:T(8,128)(2,1)S(1)} %get-tuple-element.12), kind=kOutput, calls=%fused_computation.22 | convolution fusion | flops 8600420352 | bytes 16777216 | tf_op jit(solution)/shard_map/dot_general | solution.py:79
  477.4 9.3 convolution_convert_fusion.5
  486.7 39.1 %reduce-scatter.10.cloned.1.call-done = bf16[128,2048]{1,0:T(8,128)(2,1)} async-done(((bf16[1024,2048]{1,0:T(8,128)(2,1)}), bf16[128,2048]{1,0:T(8,128)(2,1)}) %reduce-scatter.10.cloned.1.call-update) | async-done | bytes 524304 | tf_op jit(solution)/shard_map/reduce_scatter | solution.py:95
  527.2 49.3 %reduce-scatter.8.cloned.1.call-done = bf16[128,2048]{1,0:T(8,128)(2,1)} async-done(((bf16[1024,2048]{1,0:T(8,128)(2,1)}), bf16[128,2048]{1,0:T(8,128)(2,1)}) %reduce-scatter.8.cloned.1.call-update) | async-done | bytes 524304 | tf_op jit(solution)/shard_map/reduce_scatter | solution.py:95
  579.2 7.1 convolution_convert_fusion.7
  592.6 15.3 %all-to-all-done.2 = bf16[8,128,256]{1,2,0:T(8,128)(2,1)} async-done(((bf16[8,128,256]{1,2,0:T(8,128)(2,1)}), bf16[8,128,256]{1,2,0:T(8,128)(2,1)}, u32[]{:S(2)}, u32[]{:S(2)}) %all-to-all-start.2) | async-done | bytes 524320 | tf_op jit(solution)/shard_map/all_to_all | solution.py:193
  636.5 14.0 %convolution_convert_fusion = bf16[2048,2048]{1,0:T(8,128)(2,1)} fusion(bf16[1024,2048]{1,0:T(8,128)(2,1)} %all-gather.14.cloned.1.call-done, bf16[1024,1024]{1,0:T(8,128)(2,1)} %copy-done.25, bf16[1024,1024]{1,0:T(8,128)(2,1)} %copy-done.24), kind=kOutput, calls=%fused_computation.5 | convolution fusion | flops 8602517504 | bytes 16777216 | tf_op jit(solution)/shard_map/dot_general | solution.py:85
  650.5 9.6 convolution_convert_fusion.4
  660.4 7.6 convolution_convert_fusion.3
  683.7 84.8 %reduce-scatter.18.cloned.1.call-done = bf16[512,2048]{1,0:T(8,128)(2,1)} async-done(((bf16[2048,2048]{1,0:T(8,128)(2,1)}), bf16[512,2048]{1,0:T(8,128)(2,1)}) %reduce-scatter.18.cloned.1.call-update) | async-done | bytes 2097168 | tf_op jit(solution)/shard_map/reduce_scatter | solution.py:95
  773.4 50.6 %reduce-scatter.20.cloned.1.call-done = bf16[256,2048]{1,0:T(8,128)(2,1)} async-done(((bf16[1024,2048]{1,0:T(8,128)(2,1)}), bf16[256,2048]{1,0:T(8,128)(2,1)}) %reduce-scatter.20.cloned.1.call-update) | async-done | bytes 1048592 | tf_op jit(solution)/shard_map/reduce_scatter | solution.py:95
  832.8 44.0 %reduce-scatter.12.cloned.1.call-done = bf16[128,2048]{1,0:T(8,128)(2,1)} async-done(((bf16[1024,2048]{1,0:T(8,128)(2,1)}), bf16[128,2048]{1,0:T(8,128)(2,1)}) %reduce-scatter.12.cloned.1.call-update) | async-done | bytes 524304 | tf_op jit(solution)/shard_map/reduce_scatter | solution.py:95
  889.6 141.2 %reduce-scatter.16.cloned.1.call-done = bf16[64,2048]{1,0:T(8,128)(2,1)} async-done(((bf16[2048,2048]{1,0:T(8,128)(2,1)}), bf16[64,2048]{1,0:T(8,128)(2,1)}) %reduce-scatter.16.cloned.1.call-update) | async-done | bytes 262160 | tf_op jit(solution)/shard_map/reduce_scatter | solution.py:95
  (188 shorter events, 136.7 us)
Async XLA Ops:
  7.2 92.4 %all-gather.10.cloned.1.call-start = ((), (), s32[]{:S(2)}) async-start(), calls=%async_computation.13 | async-start | bytes 3932160 | tf_op jit(solution)/shard_map/all_gather | solution.py:91
  37.7 92.0 %all-gather.8.cloned.1.call-start = ((), (), s32[]{:S(2)}) async-start(), calls=%async_computation.12 | async-start | bytes 4718592 | tf_op jit(solution)/shard_map/all_gather | solution.py:91
  40.0 170.2 %all-gather.12.cloned.1.call-start = ((), (), s32[]{:S(2)}) async-start(), calls=%async_computation.14 | async-start | bytes 8650752 | tf_op jit(solution)/shard_map/all_gather | solution.py:91
  40.8 257.9 %all-gather.16.cloned.1.call-start = ((), (), s32[]{:S(2)}) async-start(), calls=%async_computation.16 | async-start | bytes 10485760 | tf_op jit(solution)/shard_map/all_gather | solution.py:91
  95.3 252.2 %all-gather.14.cloned.1.call-start = ((), (), s32[]{:S(2)}) async-start(), calls=%async_computation.15 | async-start | bytes 4718592 | tf_op jit(solution)/shard_map/all_gather | solution.py:91
  148.4 19.4 %collective-permute-start.5 = (bf16[1,128,256]{2,1,0:T(8,128)(2,1)S(1)}, bf16[1,128,256]{2,1,0:T(8,128)(2,1)S(1)}, u32[]{:S(2)}, u32[]{:S(2)}) collective-permute-start(bf16[1,128,256]{2,1,0:T(8,128)(2,1)S(1)} %bitcast.172), channel_id=1, source_target_pairs={{0,6},{1,7},{2,0},{3,1},{4,2},{5,3},{6,4},{7,5},{8,14},{9,15},{10,... | collective-permute-start | bytes 196616 | tf_op jit(solution)/shard_map/ppermute | solution.py:162
  149.9 5.7 collective-permute-start
  149.9 6.9 collective-permute-start.1
  150.5 17.2 %collective-permute-start.2 = (bf16[1,128,256]{2,1,0:T(8,128)(2,1)S(1)}, bf16[1,128,256]{2,1,0:T(8,128)(2,1)S(1)}, u32[]{:S(2)}, u32[]{:S(2)}) collective-permute-start(bf16[1,128,256]{2,1,0:T(8,128)(2,1)S(1)} %bitcast.174), channel_id=1, source_target_pairs={{0,3},{1,4},{2,5},{3,6},{4,7},{5,0},{6,1},{7,2},{8,11},{9,12},{10,... | collective-permute-start | bytes 196616 | tf_op jit(solution)/shard_map/ppermute | solution.py:162
  151.7 16.0 %collective-permute-start.3 = (bf16[1,128,256]{2,1,0:T(8,128)(2,1)S(1)}, bf16[1,128,256]{2,1,0:T(8,128)(2,1)S(1)}, u32[]{:S(2)}, u32[]{:S(2)}) collective-permute-start(bf16[1,128,256]{2,1,0:T(8,128)(2,1)S(1)} %bitcast.173), channel_id=1, source_target_pairs={{0,4},{1,5},{2,6},{3,7},{4,0},{5,1},{6,2},{7,3},{8,12},{9,13},{10,... | collective-permute-start | bytes 196616 | tf_op jit(solution)/shard_map/ppermute | solution.py:162
  155.5 12.3 %collective-permute-start.4 = (bf16[1,128,256]{2,1,0:T(8,128)(2,1)S(1)}, bf16[1,128,256]{2,1,0:T(8,128)(2,1)S(1)}, u32[]{:S(2)}, u32[]{:S(2)}) collective-permute-start(bf16[1,128,256]{2,1,0:T(8,128)(2,1)S(1)} %bitcast.171), channel_id=1, source_target_pairs={{0,5},{1,6},{2,7},{3,0},{4,1},{5,2},{6,3},{7,4},{8,13},{9,14},{10,... | collective-permute-start | bytes 196616 | tf_op jit(solution)/shard_map/ppermute | solution.py:162
  156.7 13.8 %collective-permute-start.6 = (bf16[1,128,256]{2,1,0:T(8,128)(2,1)S(1)}, bf16[1,128,256]{2,1,0:T(8,128)(2,1)S(1)}, u32[]{:S(2)}, u32[]{:S(2)}) collective-permute-start(bf16[1,128,256]{2,1,0:T(8,128)(2,1)S(1)} %bitcast.170), channel_id=1, source_target_pairs={{0,7},{1,0},{2,1},{3,2},{4,3},{5,4},{6,5},{7,6},{8,15},{9,8},{10,9... | collective-permute-start | bytes 196616 | tf_op jit(solution)/shard_map/ppermute | solution.py:162
  216.3 184.4 %all-gather.18.cloned.1.call-start = ((), (), s32[]{:S(2)}) async-start(), calls=%async_computation.17 | async-start | bytes 5242880 | tf_op jit(solution)/shard_map/all_gather | solution.py:91
  216.8 232.3 %all-gather.20.cloned.1.call-start = ((), (), s32[]{:S(2)}) async-start(), calls=%async_computation.19 | async-start | bytes 4718592 | tf_op jit(solution)/shard_map/all_gather | solution.py:91
  217.6 308.2 %reduce-scatter.10.cloned.1.call-start = ((), (), s32[]{:S(2)}) async-start(), calls=%async_computation.20 | async-start | bytes 4718592 | tf_op jit(solution)/shard_map/reduce_scatter | solution.py:95
  476.9 99.6 %reduce-scatter.8.cloned.1.call-start = ((), (), s32[]{:S(2)}) async-start(), calls=%async_computation.18 | async-start | bytes 4718592 | tf_op jit(solution)/shard_map/reduce_scatter | solution.py:95
  588.4 19.5 %all-to-all-start.2 = ((bf16[8,128,256]{1,2,0:T(8,128)(2,1)}), bf16[8,128,256]{1,2,0:T(8,128)(2,1)}, u32[]{:S(2)}, u32[]{:S(2)}) async-start(bf16[8,128,256]{1,2,0:T(8,128)(2,1)} %bitcast.157), calls=%async_computation.4 | async-start | bytes 1048576 | tf_op jit(solution)/shard_map/all_to_all | solution.py:193
  592.6 86.6 %reduce-scatter.14.cloned.1.call-start = ((), (), s32[]{:S(2)}) async-start(), calls=%async_computation.22 | async-start | bytes 3932160 | tf_op jit(solution)/shard_map/reduce_scatter | solution.py:95
  636.2 132.3 %reduce-scatter.18.cloned.1.call-start = ((), (), s32[]{:S(2)}) async-start(), calls=%async_computation.24 | async-start | bytes 10485760 | tf_op jit(solution)/shard_map/reduce_scatter | solution.py:95
  650.5 173.5 %reduce-scatter.20.cloned.1.call-start = ((), (), s32[]{:S(2)}) async-start(), calls=%async_computation.25 | async-start | bytes 5242880 | tf_op jit(solution)/shard_map/reduce_scatter | solution.py:95
  660.1 216.7 %reduce-scatter.12.cloned.1.call-start = ((), (), s32[]{:S(2)}) async-start(), calls=%async_computation.21 | async-start | bytes 4718592 | tf_op jit(solution)/shard_map/reduce_scatter | solution.py:95
  668.0 362.9 %reduce-scatter.16.cloned.1.call-start = ((), (), s32[]{:S(2)}) async-start(), calls=%async_computation.23 | async-start | bytes 8650752 | tf_op jit(solution)/shard_map/reduce_scatter | solution.py:95
  679.1 89.4 %all-to-all-start.3 = ((bf16[8,64,768]{2,1,0:T(8,128)(2,1)}), bf16[8,64,768]{2,1,0:T(8,128)(2,1)S(1)}, u32[]{:S(2)}, u32[]{:S(2)}) async-start(bf16[8,64,768]{2,1,0:T(8,128)(2,1)} %bitcast.161), calls=%async_computation.7 | async-start | bytes 1572864 | tf_op jit(solution)/shard_map/all_to_all | solution.py:110
  768.5 112.2 %all-to-all-start.4 = ((bf16[8,64,2048]{2,1,0:T(8,128)(2,1)}), bf16[8,64,2048]{2,1,0:T(8,128)(2,1)}, u32[]{:S(2)}, u32[]{:S(2)}) async-start(bf16[8,64,2048]{2,1,0:T(8,128)(2,1)} %bitcast.156), calls=%async_computation.10 | async-start | bytes 4194304 | tf_op jit(solution)/shard_map/all_to_all | solution.py:110
  (26 other events, 365.4 us)
Sparse Core Ops, SparseCore 0:
  37.8 42.7 all-gather.9
  82.8 46.8 all-gather.7
  132.7 77.5 all-gather.11
  212.5 86.0 all-gather.15
  300.7 46.8 all-gather.13
  349.3 51.3 all-gather.17
  402.3 46.8 all-gather.19
  477.0 48.7 reduce-scatter.9
  528.1 48.3 reduce-scatter.7
  636.4 42.7 reduce-scatter.13
  682.2 86.2 reduce-scatter.17
  771.3 52.6 reduce-scatter.19
  826.9 49.8 reduce-scatter.11
  879.0 151.8 reduce-scatter.15
